TPU v7x, 32 devices: a whole 2x2x4 slice. The times are simulated.
32 devices in a mesh: ctx: 8 (over z, x), head: 4 (over y, core).
Axes of the slice: x: 2, y: 2, z: 4, core: 2. Of those that a mesh axis runs over, the one named last changes fastest.
Arguments:
- query_nope: bfloat16 [256, 16384], P('head'), may hold values from -6 to 6
- query_rope: bfloat16 [256, 8192], P('head'), may hold values from -10 to 10
- latent_cache: bfloat16 [4096, 512], P('ctx'), may hold values from -6 to 6
- rope_keys: bfloat16 [64, 4096], P(None, 'ctx'), may hold values from -6 to 6
- absorb_keys: bfloat16 [128, 128, 512], P('head'), may hold values from -0.5 to 0.5
- expand_values: bfloat16 [128, 512, 128], P('head'), may hold values from -2.09375 to 2.09375
- block_ids: int32 [128, 2, 16], P('head'), may hold values from -1 to 31, as said below
- block_counts: int32 [128, 2], P('head'), may hold values from 8 to 16
Outputs:
- attended: bfloat16 [256, 16384], P('head')
Inputs may be any that keep to these rules, and one draw needn't show every extreme that they name: `block_ids`: entries beyond block_counts are -1; the first block_counts entries are distinct blocks, none after the query block's own block 30 + q, and entry 0 is that own block.
All inputs are finite; a program needn't handle non-finite values.
Results may differ from a plain program's by a relative error of at most 0.0066.
Values may be sent and summed in bfloat16 or wider, within the bound.
No kernel may reach another device: no remote copies, remote signals or barrier semaphores. Data moves between devices by JAX's collectives and lax.ppermute only.
A program may use at most 128 MiB of HBM per device.

v0:
```python
import math
import jax
import jax.numpy as jnp
from jax import lax
from jax.sharding import PartitionSpec as P

BLOCK = 128


def body(
    query_nope,
    query_rope,
    latent_cache,
    rope_keys,
    absorb_keys,
    expand_values,
    block_ids,
    block_counts,
):
    nope_all, rope_all = (
        lax.all_to_all(query_nope, "head", split_axis=1, concat_axis=0, tiled=True),
        lax.all_to_all(query_rope, "head", split_axis=1, concat_axis=0, tiled=True),
    )
    tokens = nope_all.shape[0]
    heads_here = absorb_keys.shape[0]
    nope_width = absorb_keys.shape[1]
    rope_width = rope_keys.shape[0]
    value_width = expand_values.shape[2]
    keys_here = latent_cache.shape[0]
    blocks_here = keys_here // BLOCK
    query_blocks = tokens // BLOCK
    slot_count = block_ids.shape[2]
    shards = lax.axis_size("ctx")
    ctx_index = lax.axis_index("ctx")
    score_scale = 1.0 / math.sqrt(nope_width + rope_width)
    query_latent = jnp.einsum(
        "thn,hnl->htl",
        nope_all.reshape(tokens, heads_here, nope_width),
        absorb_keys,
        preferred_element_type=jnp.float32,
    ).astype(jnp.bfloat16)
    scores = jnp.einsum(
        "htl,kl->htk", query_latent, latent_cache, preferred_element_type=jnp.float32
    )
    scores = scores + jnp.einsum(
        "thr,rk->htk",
        rope_all.reshape(tokens, heads_here, rope_width),
        rope_keys,
        preferred_element_type=jnp.float32,
    )
    scores = (scores * score_scale).reshape(heads_here, query_blocks, BLOCK, blocks_here, BLOCK)
    block_global = ctx_index * blocks_here + jnp.arange(blocks_here, dtype=jnp.int32)
    slot_live = jnp.arange(slot_count, dtype=jnp.int32)[None, None, :] < block_counts[:, :, None]
    chosen = jnp.any((block_ids[..., None] == block_global) & slot_live[..., None], axis=2)
    query_pos = keys_here * shards - tokens + jnp.arange(tokens, dtype=jnp.int32)
    key_pos = ctx_index * keys_here + jnp.arange(keys_here, dtype=jnp.int32)
    causal = (key_pos[None, :] <= query_pos[:, None]).reshape(
        query_blocks, BLOCK, blocks_here, BLOCK
    )
    allowed = chosen[:, :, None, :, None] & causal[None]
    local_top = jnp.max(jnp.where(allowed, scores, -1e30), axis=(3, 4))
    weights = jnp.where(allowed, jnp.exp(scores - local_top[..., None, None]), 0.0).astype(
        jnp.bfloat16
    )
    weights = weights.reshape(heads_here, tokens, keys_here)
    top_rows = local_top.reshape(heads_here, tokens).T
    weight_total = jnp.sum(weights, axis=2, dtype=jnp.float32).T
    latent_sum = jnp.einsum(
        "htk,kl->thl", weights, latent_cache, preferred_element_type=jnp.float32
    )
    value_float = expand_values.astype(jnp.float32)
    per_device = tokens // shards
    partial_out = jnp.einsum(
        "thl,hlv->thv", latent_sum, value_float, precision=lax.Precision.HIGHEST
    )
    parts_out, parts_total, parts_top = (
        lax.all_to_all(partial_out[None], "ctx", split_axis=1, concat_axis=0, tiled=True),
        lax.all_to_all(weight_total[None], "ctx", split_axis=1, concat_axis=0, tiled=True),
        lax.all_to_all(top_rows[None], "ctx", split_axis=1, concat_axis=0, tiled=True),
    )
    best = jnp.max(parts_top, axis=0)
    factor = jnp.exp(parts_top - best[None])
    summed_out = jnp.sum(parts_out * factor[..., None], axis=0)
    summed_total = jnp.sum(parts_total * factor, axis=0)
    rows_done = (
        (summed_out / summed_total[..., None])
        .astype(jnp.bfloat16)
        .reshape(per_device, heads_here * value_width)
    )
    merged = lax.all_gather(rows_done, "ctx", axis=0, tiled=True)
    return lax.all_to_all(merged, "head", split_axis=0, concat_axis=1, tiled=True)


def solution(mesh):
    return jax.shard_map(
        body,
        mesh=mesh,
        in_specs=(
            P("head", None),
            P("head", None),
            P("ctx", None),
            P(None, "ctx"),
            P("head", None, None),
            P("head", None, None),
            P("head", None, None),
            P("head", None),
        ),
        out_specs=P("head", None),
        check_vma=False,
    )
```

profile of v0, /device:TPU:0, one launch (start us, length us, event | category | flops | bytes accessed | tf_op | source)
XLA Modules:
  0.0 328.8 jit_solution(10380978903736725854)
XLA Ops:
  6.5 0.0 copy-start
  6.5 2.4 copy.105
  8.9 4.3 %all-to-all-start.1 = ((bf16[64,4,2048]{2,0,1:T(8,128)(2,1)}), bf16[64,4,2048]{2,0,1:T(8,128)(2,1)S(1)}, u32[]{:S(2)}, u32[]{:S(2)}) async-start(bf16[64,4,2048]{2,0,1:T(8,128)(2,1)} %bitcast.63), calls=%async_computation.1 | async-start | bytes 2097152 | tf_op jit(solution)/shard_map/all_to_all | solution.py:22
  13.2 0.0 copy-start.5
  13.2 0.0 copy-start.4
  13.2 3.2 copy.104
  16.3 11.3 %all-to-all-done.1 = bf16[64,4,2048]{2,0,1:T(8,128)(2,1)S(1)} async-done(((bf16[64,4,2048]{2,0,1:T(8,128)(2,1)}), bf16[64,4,2048]{2,0,1:T(8,128)(2,1)S(1)}, u32[]{:S(2)}, u32[]{:S(2)}) %all-to-all-start.1) | async-done | bytes 1048608 | tf_op jit(solution)/shard_map/all_to_all | solution.py:22
  27.6 0.0 copy-start.2
  27.6 4.4 %all-to-all-start = ((bf16[64,4,4096]{2,0,1:T(8,128)(2,1)}), bf16[64,4,4096]{2,0,1:T(8,128)(2,1)}, u32[]{:S(2)}, u32[]{:S(2)}) async-start(bf16[64,4,4096]{2,0,1:T(8,128)(2,1)} %bitcast.62), calls=%async_computation | async-start | bytes 4194304 | tf_op jit(solution)/shard_map/all_to_all | solution.py:21
  32.1 0.0 copy-done.5
  32.1 0.0 copy-done.4
  32.1 0.1 and_reduce_fusion
  32.2 0.1 copy.70
  32.3 4.2 %and.28 = pred[32,2,128,4,128]{4,3,2,1,0:T(4,128)(4,1)} broadcast(pred[32,2,4]{2,1,0:T(4,128)(4,1)S(1)} %copy.70), dimensions={0,1,3} | broadcast | bytes 4194560 | tf_op jit(solution)/shard_map/and | solution.py:60
  36.5 0.0 copy-done.2
  36.5 0.0 copy-start.3
  36.5 14.4 %and.29 = pred[32,256,512]{2,1,0:T(32,128)(4,1)} reshape(pred[32,2,128,4,128]{4,3,2,1,0:T(4,128)(4,1)} %and.28) | data formatting | bytes 8388608 | tf_op jit(solution)/shard_map/and | solution.py:60
  50.9 0.1 broadcast_compare_fusion
  51.0 3.3 %reshape.108 = bf16[256,32,64]{2,1,0:T(8,128)(2,1)S(1)} reshape(bf16[4,64,2048]{2,1,0:T(8,128)(2,1)} %bitcast.66) | data formatting | bytes 2097152 | tf_op jit(solution)/shard_map/reshape | solution.py:47
  54.4 0.0 copy-done.3
  54.4 8.0 %fusion.10 = f32[512,256,32]{0,1,2:T(8,128)} fusion(bf16[256,32,64]{2,1,0:T(8,128)(2,1)S(1)} %reshape.108, bf16[64,512]{1,0:T(8,128)(2,1)S(1)} %copy-done.3), kind=kOutput, calls=%fused_computation.13 | convolution fusion | flops 536870912 | bytes 17891328 | tf_op jit(solution)/shard_map/thr,rk->htk/dot_general | solution.py:45
  62.4 0.0 all-to-all-done
  62.4 2.1 copy.90
  64.5 0.0 copy-done
  64.5 17.7 %select_reduce_fusion = (f32[32,256]{1,0:T(8,128)S(1)}, f32[32,256,512]{2,1,0:T(8,128)}) fusion(pred[32,256,512]{2,1,0:T(32,128)(4,1)} %and.29, pred[256,512]{1,0:T(8,128)(4,1)S(1)} %broadcast_compare_fusion, f32[512,256,32]{0,1,2:T(8,128)} %fusion.10, bf16[512,512]{1,0:T(8,128)(2,1)S(1)} %copy-done, bf16[32,128,512]{2,1,0:T(8,128)(2,1)} %param.12, ...), kind=kOutput, calls=%fused_computation.6 | convolution fusion | flops 5393866752 | bytes 44728320 | tf_op jit(solution)/shard_map/htl,kl->htk/dot_general | solution.py:42
  82.2 9.9 %convert_reduce_fusion = f32[32,256]{1,0:T(8,128)S(1)} fusion(f32[32,256,512]{2,1,0:T(8,128)} %get-tuple-element.8, f32[32,256]{1,0:T(8,128)S(1)} %get-tuple-element.7, pred[32,256,512]{2,1,0:T(32,128)(4,1)} %and.29, pred[256,512]{1,0:T(8,128)(4,1)S(1)} %broadcast_compare_fusion), kind=kLoop, calls=%fused_computation.4 | loop fusion | flops 25157632 | bytes 21168128 | tf_op jit(solution)/shard_map/reduce_sum | solution.py:67
  92.0 0.1 copy.81
  92.1 0.5 broadcast.83
  92.7 0.9 reduce.1
  93.6 0.7 reshape.113
  94.4 6.5 %all-to-all-start.4 = ((f32[8,1,1024]{2,1,0:T(1,128)}), f32[8,1,1024]{2,1,0:T(1,128)S(1)}, u32[]{:S(2)}, u32[]{:S(2)}) async-start(f32[8,1,1024]{2,1,0:T(1,128)} %reshape.113), calls=%async_computation.4 | async-start | bytes 65536 | tf_op jit(solution)/shard_map/all_to_all | solution.py:78
  100.9 12.9 %fusion.14 = f32[32,256,512]{2,1,0:T(8,128)} fusion(bf16[512,512]{1,0:T(8,128)(2,1)S(1)} %copy-done, f32[32,256,512]{2,1,0:T(8,128)} %get-tuple-element.8, pred[32,256,512]{2,1,0:T(32,128)(4,1)} %and.29, f32[32,256]{1,0:T(8,128)S(1)} %get-tuple-element.7, pred[256,512]{1,0:T(8,128)(4,1)S(1)} %broadcast_compare_fusion), kind=kOutput, calls=%fused_computation.17 | convolution fusion | flops 4311744512 | bytes 38436864 | tf_op jit(solution)/shard_map/htk,kl->thl/dot_general | solution.py:68
  113.8 0.1 copy.77
  113.8 0.9 reduce.3
  114.8 0.7 reshape.111
  115.5 0.0 all-to-all-done.4
  115.5 6.0 %all-to-all-start.3 = ((f32[8,1,1024]{2,1,0:T(1,128)}), f32[8,1,1024]{2,1,0:T(1,128)S(1)}, u32[]{:S(2)}, u32[]{:S(2)}) async-start(f32[8,1,1024]{2,1,0:T(1,128)} %reshape.111), calls=%async_computation.3 | async-start | bytes 65536 | tf_op jit(solution)/shard_map/all_to_all | solution.py:79
  121.5 13.2 %fusion.7 = f32[1,256,32,128]{3,1,2,0:T(8,128)S(1)} fusion(bf16[32,512,128]{2,1,0:T(8,128)(2,1)} %param.13, f32[32,256,512]{2,1,0:T(8,128)} %fusion.14), kind=kOutput, calls=%fused_computation.11 | convolution fusion | flops 6442450944 | bytes 25165824 | tf_op jit(solution)/shard_map/thl,hlv->thv/dot_general | solution.py:73
  134.7 4.4 %copy.76 = f32[1,256,32,128]{3,2,0,1:T(8,128)} copy(f32[1,256,32,128]{3,1,2,0:T(8,128)S(1)} %fusion.7) | data formatting | bytes 8388608 | tf_op jit(solution)/shard_map/broadcast_in_dim | solution.py:77
  139.1 0.0 all-to-all-done.3
  139.1 6.0 %all-to-all-start.2 = ((f32[1,256,32,128]{3,2,0,1:T(8,128)}), f32[1,256,32,128]{3,2,0,1:T(8,128)}, u32[]{:S(2)}, u32[]{:S(2)}) async-start(f32[1,256,32,128]{3,2,0,1:T(8,128)} %copy.76), calls=%async_computation.2 | async-start | bytes 8388608 | tf_op jit(solution)/shard_map/all_to_all | solution.py:77
  145.1 0.0 all-gather.2.cloned.1.call-start
  145.1 0.7 reduce.2
  145.8 0.2 reshape.114
  146.1 0.1 copy.82
  146.2 0.7 reduce.4
  146.9 0.2 reshape.112
  147.1 0.1 copy.79
  147.2 0.1 copy.78
  147.3 0.1 multiply_reduce_fusion
  147.4 90.5 %all-to-all-done.2 = f32[1,256,32,128]{3,2,0,1:T(8,128)} async-done(((f32[1,256,32,128]{3,2,0,1:T(8,128)}), f32[1,256,32,128]{3,2,0,1:T(8,128)}, u32[]{:S(2)}, u32[]{:S(2)}) %all-to-all-start.2) | async-done | bytes 4194336 | tf_op jit(solution)/shard_map/all_to_all | solution.py:77
  237.8 3.9 %fusion.6 = f32[32,32,128]{2,0,1:T(8,128)S(1)} fusion(f32[8,32,32,128]{3,2,1,0:T(8,128)} %bitcast.10, f32[8,32,32]{1,0,2:T(8,128)S(1)} %get-tuple-element.6), kind=kLoop, calls=%fused_computation.10 | loop fusion | flops 1966080 | bytes 4751360 | tf_op jit(solution)/shard_map/reduce_sum | solution.py:83
  241.8 0.9 copy_bitcast_fusion.2
  242.7 0.0 all-gather.2.cloned.1.call-update
  242.7 48.4 %all-gather.2.cloned.1.call-done = bf16[256,4096]{1,0:T(8,128)(2,1)} async-done(((bf16[32,4096]{1,0:T(8,128)(2,1)}), bf16[256,4096]{1,0:T(8,128)(2,1)}) %all-gather.2.cloned.1.call-update) | async-done | bytes 2097168 | tf_op jit(solution)/shard_map/all_gather | solution.py:90
  291.2 0.0 copy-start.1
  291.2 29.4 %all_to_all.87 = bf16[4,64,4096]{2,1,0:T(8,128)(2,1)S(1)} all-to-all(bf16[4,64,4096]{2,1,0:T(8,128)(2,1)} %bitcast.68), channel_id=1, replica_groups=mesh['ctx'=8,'head'=4] {'head'}, dimensions={0} | all-to-all | bytes 4194304 | tf_op jit(solution)/shard_map/all_to_all | solution.py:91
  320.5 1.5 copy.89
  322.0 0.0 copy-done.1
  (5 shorter events, 0.0 us)
Async XLA Ops:
  6.5 58.0 %copy-start = (bf16[512,512]{1,0:T(8,128)(2,1)S(1)}, bf16[512,512]{1,0:T(8,128)(2,1)}, u32[]{:S(2)}) copy-start(bf16[512,512]{1,0:T(8,128)(2,1)} %param.10) | copy-start | bytes 1572868
  8.9 18.7 %all-to-all-start.1 = ((bf16[64,4,2048]{2,0,1:T(8,128)(2,1)}), bf16[64,4,2048]{2,0,1:T(8,128)(2,1)S(1)}, u32[]{:S(2)}, u32[]{:S(2)}) async-start(bf16[64,4,2048]{2,0,1:T(8,128)(2,1)} %bitcast.63), calls=%async_computation.1 | async-start | bytes 2097152 | tf_op jit(solution)/shard_map/all_to_all | solution.py:22
  13.2 18.9 %copy-start.5 = (s32[32,2]{0,1:T(2,128)S(1)}, s32[32,2]{0,1:T(2,128)}, u32[]{:S(2)}) copy-start(s32[32,2]{0,1:T(2,128)} %param.15) | copy-start | bytes 772
  13.2 18.9 %copy-start.4 = (s32[32,2,16]{0,2,1:T(8,128)S(1)}, s32[32,2,16]{0,2,1:T(8,128)}, u32[]{:S(2)}) copy-start(s32[32,2,16]{0,2,1:T(8,128)} %param.14) | copy-start | bytes 12292
  27.6 8.9 %copy-start.2 = (bf16[64,4,2048]{2,0,1:T(8,128)(2,1)}, bf16[64,4,2048]{2,0,1:T(8,128)(2,1)S(1)}, u32[]{:S(2)}) copy-start(bf16[64,4,2048]{2,0,1:T(8,128)(2,1)S(1)} %all-to-all-done.1) | copy-start | bytes 3145732
  27.6 34.8 %all-to-all-start = ((bf16[64,4,4096]{2,0,1:T(8,128)(2,1)}), bf16[64,4,4096]{2,0,1:T(8,128)(2,1)}, u32[]{:S(2)}, u32[]{:S(2)}) async-start(bf16[64,4,4096]{2,0,1:T(8,128)(2,1)} %bitcast.62), calls=%async_computation | async-start | bytes 4194304 | tf_op jit(solution)/shard_map/all_to_all | solution.py:21
  36.5 17.9 %copy-start.3 = (bf16[64,512]{1,0:T(8,128)(2,1)S(1)}, bf16[64,512]{1,0:T(8,128)(2,1)}, u32[]{:S(2)}) copy-start(bf16[64,512]{1,0:T(8,128)(2,1)} %param.11) | copy-start | bytes 196612
  94.4 21.2 %all-to-all-start.4 = ((f32[8,1,1024]{2,1,0:T(1,128)}), f32[8,1,1024]{2,1,0:T(1,128)S(1)}, u32[]{:S(2)}, u32[]{:S(2)}) async-start(f32[8,1,1024]{2,1,0:T(1,128)} %reshape.113), calls=%async_computation.4 | async-start | bytes 65536 | tf_op jit(solution)/shard_map/all_to_all | solution.py:78
  115.5 23.6 %all-to-all-start.3 = ((f32[8,1,1024]{2,1,0:T(1,128)}), f32[8,1,1024]{2,1,0:T(1,128)S(1)}, u32[]{:S(2)}, u32[]{:S(2)}) async-start(f32[8,1,1024]{2,1,0:T(1,128)} %reshape.111), calls=%async_computation.3 | async-start | bytes 65536 | tf_op jit(solution)/shard_map/all_to_all | solution.py:79
  139.1 98.8 %all-to-all-start.2 = ((f32[1,256,32,128]{3,2,0,1:T(8,128)}), f32[1,256,32,128]{3,2,0,1:T(8,128)}, u32[]{:S(2)}, u32[]{:S(2)}) async-start(f32[1,256,32,128]{3,2,0,1:T(8,128)} %copy.76), calls=%async_computation.2 | async-start | bytes 8388608 | tf_op jit(solution)/shard_map/all_to_all | solution.py:77
  145.1 146.1 %all-gather.2.cloned.1.call-start = ((), (), s32[]{:S(2)}) async-start(), calls=%async_computation.6 | async-start | bytes 2359296 | tf_op jit(solution)/shard_map/all_gather | solution.py:90
  291.2 30.8 %copy-start.1 = (bf16[512,512]{1,0:T(8,128)(2,1)S(1)}, bf16[512,512]{1,0:T(8,128)(2,1)}, u32[]{:S(2)}) copy-start(bf16[512,512]{1,0:T(8,128)(2,1)} %param.10) | copy-start | bytes 1572868
Sparse Core Ops, SparseCore 0:
  242.8 48.2 all-gather.1
where the time goes:
time: 330 us; the launch traced here: 329 us
  waiting for transfers between devices  150 us (45%)
  matrix products  51.8 us (16%)
  local copies, waits for them, and re-layouts  38.3 us (12%)
  blocking collectives  29.4 us (9%)
  starting transfers between devices  27.2 us (8%)
  other arithmetic  18.3 us (6%)
  between operations  13.6 us (4%)
    all_to_all x1, waiting for transfers between devices, body(): lax.all_to_all(partial_out[None], 'ctx', split_axis=1, concat_axis=0, til...  90.5 us
    all_gather x1, waiting for transfers between devices, body(): merged = lax.all_gather(rows_done, 'ctx', axis=0, tiled=True)  48.4 us
    all_to_all x1, blocking collectives, body(): lax.all_to_all(merged, 'head', split_axis=0, concat_axis=1, tiled=True)  29.4 us
    and x2, local copies, waits for them, and re-layouts, body(): allowed = chosen[:, :, None, :, None] & causal[None]  18.5 us
    dot_general x1, matrix products, body(): jnp.einsum('htl,kl->htk', query_latent, latent_cache, preferred_element_t...  17.7 us
    dot_general x1, matrix products, body(): jnp.einsum('thl,hlv->thv', latent_sum, value_float, precision=lax.Precisi...  13.2 us
    dot_general x1, matrix products, body(): jnp.einsum('htk,kl->thl', weights, latent_cache, preferred_element_type=j...  12.9 us
    all_to_all x1, waiting for transfers between devices, body(): lax.all_to_all(query_rope, 'head', split_axis=1, concat_axis=0, tiled=True)  11.3 us
  transfers between devices with their start and end apart: 6, of which 3 were waited for; matrix products, arithmetic and copies ran while one was open for 21% of the time, Pallas kernels for 0%

commit v1 on v0

--- a/solution.py
+++ b/solution.py
@@ -87,7 +87,9 @@
         .astype(jnp.bfloat16)
         .reshape(per_device, heads_here * value_width)
     )
-    merged = lax.all_gather(rows_done, "ctx", axis=0, tiled=True)
+    merged = jnp.concatenate(
+        lax.all_to_all(jnp.stack([rows_done] * lax.axis_size("ctx")), "ctx", 0, 0), axis=0
+    )
     return lax.all_to_all(merged, "head", split_axis=0, concat_axis=1, tiled=True)
 
 

time: 330 us -> 319 us (0.967)
  blocking collectives: 29.4 us -> 80.3 us
  waiting for transfers between devices: 150 us -> 102 us
  between operations: 13.6 us -> 0.22 us
    all_to_all x0 -> x1, blocking collectives: none -> 51.8 us  [body(): lax.all_to_all(jnp.stack([rows_done] * lax.axis_size('ctx')), 'ctx', 0, 0)]
    all_gather x1 -> x0, waiting for transfers between devices: 48.4 us -> none  [body(): merged = lax.all_gather(rows_done, 'ctx', axis=0, tiled=True)]
  transfers between devices with their start and end apart: 6 -> 5, of which waited for: 3 -> 2; matrix products, arithmetic and copies ran while one was open for 21% -> 21% of each run, Pallas kernels for 0% -> 0%
where the time goes in v1:
time: 319 us; the launch traced here: 317 us
  waiting for transfers between devices  102 us (32%)
  blocking collectives  80.3 us (25%)
  matrix products  51.8 us (16%)
  local copies, waits for them, and re-layouts  38.5 us (12%)
  starting transfers between devices  27.2 us (9%)
  other arithmetic  17.6 us (6%)
    all_to_all x1, waiting for transfers between devices, body(): lax.all_to_all(partial_out[None], 'ctx', split_axis=1, concat_axis=0, til...  90.5 us
    all_to_all x1, blocking collectives, body(): lax.all_to_all(jnp.stack([rows_done] * lax.axis_size('ctx')), 'ctx', 0, 0)  51.8 us
    all_to_all x1, blocking collectives, body(): lax.all_to_all(merged, 'head', split_axis=0, concat_axis=1, tiled=True)  28.5 us
    and x2, local copies, waits for them, and re-layouts, body(): allowed = chosen[:, :, None, :, None] & causal[None]  18.5 us
    dot_general x1, matrix products, body(): jnp.einsum('htl,kl->htk', query_latent, latent_cache, preferred_element_t...  17.7 us
    dot_general x1, matrix products, body(): jnp.einsum('thl,hlv->thv', latent_sum, value_float, precision=lax.Precisi...  13.2 us
    dot_general x1, matrix products, body(): jnp.einsum('htk,kl->thl', weights, latent_cache, preferred_element_type=j...  12.9 us
    all_to_all x1, waiting for transfers between devices, body(): lax.all_to_all(query_rope, 'head', split_axis=1, concat_axis=0, tiled=True)  11.3 us
  transfers between devices with their start and end apart: 5, of which 2 were waited for; matrix products, arithmetic and copies ran while one was open for 21% of the time, Pallas kernels for 0%

profile of v1, /device:TPU:0, one launch (start us, length us, event | category | flops | bytes accessed | tf_op | source)
XLA Modules:
  0.0 317.4 jit_solution(9672299922645989118)
XLA Ops:
  0.0 0.0 copy-start
  0.0 2.4 copy.105
  2.4 4.3 %all-to-all-start.1 = ((bf16[64,4,2048]{2,0,1:T(8,128)(2,1)}), bf16[64,4,2048]{2,0,1:T(8,128)(2,1)S(1)}, u32[]{:S(2)}, u32[]{:S(2)}) async-start(bf16[64,4,2048]{2,0,1:T(8,128)(2,1)} %bitcast.63), calls=%async_computation.1 | async-start | bytes 2097152 | tf_op jit(solution)/shard_map/all_to_all | solution.py:22
  6.7 0.0 copy-start.5
  6.7 0.0 copy-start.4
  6.7 3.2 copy.104
  9.8 11.3 %all-to-all-done.1 = bf16[64,4,2048]{2,0,1:T(8,128)(2,1)S(1)} async-done(((bf16[64,4,2048]{2,0,1:T(8,128)(2,1)}), bf16[64,4,2048]{2,0,1:T(8,128)(2,1)S(1)}, u32[]{:S(2)}, u32[]{:S(2)}) %all-to-all-start.1) | async-done | bytes 1048608 | tf_op jit(solution)/shard_map/all_to_all | solution.py:22
  21.1 0.0 copy-start.2
  21.1 4.4 %all-to-all-start = ((bf16[64,4,4096]{2,0,1:T(8,128)(2,1)}), bf16[64,4,4096]{2,0,1:T(8,128)(2,1)}, u32[]{:S(2)}, u32[]{:S(2)}) async-start(bf16[64,4,4096]{2,0,1:T(8,128)(2,1)} %bitcast.62), calls=%async_computation | async-start | bytes 4194304 | tf_op jit(solution)/shard_map/all_to_all | solution.py:21
  25.6 0.0 copy-done.5
  25.6 0.0 copy-done.4
  25.6 0.1 and_reduce_fusion
  25.7 0.1 copy.70
  25.8 4.2 %and.28 = pred[32,2,128,4,128]{4,3,2,1,0:T(4,128)(4,1)} broadcast(pred[32,2,4]{2,1,0:T(4,128)(4,1)S(1)} %copy.70), dimensions={0,1,3} | broadcast | bytes 4194560 | tf_op jit(solution)/shard_map/and | solution.py:60
  30.0 0.0 copy-done.2
  30.0 0.0 copy-start.3
  30.0 14.4 %and.29 = pred[32,256,512]{2,1,0:T(32,128)(4,1)} reshape(pred[32,2,128,4,128]{4,3,2,1,0:T(4,128)(4,1)} %and.28) | data formatting | bytes 8388608 | tf_op jit(solution)/shard_map/and | solution.py:60
  44.4 0.1 broadcast_compare_fusion
  44.5 3.3 %reshape.112 = bf16[256,32,64]{2,1,0:T(8,128)(2,1)S(1)} reshape(bf16[4,64,2048]{2,1,0:T(8,128)(2,1)} %bitcast.67) | data formatting | bytes 2097152 | tf_op jit(solution)/shard_map/reshape | solution.py:47
  47.9 0.0 copy-done.3
  47.9 8.0 %fusion.10 = f32[512,256,32]{0,1,2:T(8,128)} fusion(bf16[256,32,64]{2,1,0:T(8,128)(2,1)S(1)} %reshape.112, bf16[64,512]{1,0:T(8,128)(2,1)S(1)} %copy-done.3), kind=kOutput, calls=%fused_computation.13 | convolution fusion | flops 536870912 | bytes 17891328 | tf_op jit(solution)/shard_map/thr,rk->htk/dot_general | solution.py:45
  55.9 0.0 all-to-all-done
  55.9 2.1 copy.90
  58.0 0.0 copy-done
  58.0 17.7 %select_reduce_fusion = (f32[32,256]{1,0:T(8,128)S(1)}, f32[32,256,512]{2,1,0:T(8,128)}) fusion(pred[32,256,512]{2,1,0:T(32,128)(4,1)} %and.29, pred[256,512]{1,0:T(8,128)(4,1)S(1)} %broadcast_compare_fusion, f32[512,256,32]{0,1,2:T(8,128)} %fusion.10, bf16[512,512]{1,0:T(8,128)(2,1)S(1)} %copy-done, bf16[32,128,512]{2,1,0:T(8,128)(2,1)} %param.12, ...), kind=kOutput, calls=%fused_computation.6 | convolution fusion | flops 5393866752 | bytes 44728320 | tf_op jit(solution)/shard_map/htl,kl->htk/dot_general | solution.py:42
  75.7 9.9 %convert_reduce_fusion = f32[32,256]{1,0:T(8,128)S(1)} fusion(f32[32,256,512]{2,1,0:T(8,128)} %get-tuple-element.8, f32[32,256]{1,0:T(8,128)S(1)} %get-tuple-element.7, pred[32,256,512]{2,1,0:T(32,128)(4,1)} %and.29, pred[256,512]{1,0:T(8,128)(4,1)S(1)} %broadcast_compare_fusion), kind=kLoop, calls=%fused_computation.4 | loop fusion | flops 25157632 | bytes 21168128 | tf_op jit(solution)/shard_map/reduce_sum | solution.py:67
  85.5 0.1 copy.81
  85.6 0.5 broadcast.85
  86.2 0.9 reduce.1
  87.1 0.7 reshape.117
  87.8 6.5 %all-to-all-start.4 = ((f32[8,1,1024]{2,1,0:T(1,128)}), f32[8,1,1024]{2,1,0:T(1,128)S(1)}, u32[]{:S(2)}, u32[]{:S(2)}) async-start(f32[8,1,1024]{2,1,0:T(1,128)} %reshape.117), calls=%async_computation.4 | async-start | bytes 65536 | tf_op jit(solution)/shard_map/all_to_all | solution.py:78
  94.3 12.9 %fusion.14 = f32[32,256,512]{2,1,0:T(8,128)} fusion(bf16[512,512]{1,0:T(8,128)(2,1)S(1)} %copy-done, f32[32,256,512]{2,1,0:T(8,128)} %get-tuple-element.8, pred[32,256,512]{2,1,0:T(32,128)(4,1)} %and.29, f32[32,256]{1,0:T(8,128)S(1)} %get-tuple-element.7, pred[256,512]{1,0:T(8,128)(4,1)S(1)} %broadcast_compare_fusion), kind=kOutput, calls=%fused_computation.17 | convolution fusion | flops 4311744512 | bytes 38436864 | tf_op jit(solution)/shard_map/htk,kl->thl/dot_general | solution.py:68
  107.2 0.1 copy.77
  107.3 0.9 reduce.3
  108.3 0.7 reshape.115
  109.0 0.0 all-to-all-done.4
  109.0 6.0 %all-to-all-start.3 = ((f32[8,1,1024]{2,1,0:T(1,128)}), f32[8,1,1024]{2,1,0:T(1,128)S(1)}, u32[]{:S(2)}, u32[]{:S(2)}) async-start(f32[8,1,1024]{2,1,0:T(1,128)} %reshape.115), calls=%async_computation.3 | async-start | bytes 65536 | tf_op jit(solution)/shard_map/all_to_all | solution.py:79
  115.0 13.2 %fusion.7 = f32[1,256,32,128]{3,1,2,0:T(8,128)S(1)} fusion(bf16[32,512,128]{2,1,0:T(8,128)(2,1)} %param.13, f32[32,256,512]{2,1,0:T(8,128)} %fusion.14), kind=kOutput, calls=%fused_computation.11 | convolution fusion | flops 6442450944 | bytes 25165824 | tf_op jit(solution)/shard_map/thl,hlv->thv/dot_general | solution.py:73
  128.2 4.4 %copy.76 = f32[1,256,32,128]{3,2,0,1:T(8,128)} copy(f32[1,256,32,128]{3,1,2,0:T(8,128)S(1)} %fusion.7) | data formatting | bytes 8388608 | tf_op jit(solution)/shard_map/broadcast_in_dim | solution.py:77
  132.6 0.0 all-to-all-done.3
  132.6 6.0 %all-to-all-start.2 = ((f32[1,256,32,128]{3,2,0,1:T(8,128)}), f32[1,256,32,128]{3,2,0,1:T(8,128)}, u32[]{:S(2)}, u32[]{:S(2)}) async-start(f32[1,256,32,128]{3,2,0,1:T(8,128)} %copy.76), calls=%async_computation.2 | async-start | bytes 8388608 | tf_op jit(solution)/shard_map/all_to_all | solution.py:77
  138.5 0.7 reduce.2
  139.3 0.2 reshape.118
  139.5 0.1 copy.82
  139.6 0.7 reduce.4
  140.3 0.2 reshape.116
  140.5 0.1 copy.79
  140.7 0.1 copy.78
  140.7 0.1 multiply_reduce_fusion
  140.8 90.5 %all-to-all-done.2 = f32[1,256,32,128]{3,2,0,1:T(8,128)} async-done(((f32[1,256,32,128]{3,2,0,1:T(8,128)}), f32[1,256,32,128]{3,2,0,1:T(8,128)}, u32[]{:S(2)}, u32[]{:S(2)}) %all-to-all-start.2) | async-done | bytes 4194336 | tf_op jit(solution)/shard_map/all_to_all | solution.py:77
  231.3 3.9 %fusion.6 = f32[32,32,128]{2,0,1:T(8,128)S(1)} fusion(f32[8,32,32,128]{3,2,1,0:T(8,128)} %bitcast.10, f32[8,32,32]{1,0,2:T(8,128)S(1)} %get-tuple-element.6), kind=kLoop, calls=%fused_computation.10 | loop fusion | flops 1966080 | bytes 4751360 | tf_op jit(solution)/shard_map/reduce_sum | solution.py:83
  235.2 0.2 copy_bitcast_fusion.2
  235.4 0.2 stack.3
  235.7 51.8 %all_to_all.92 = bf16[8,32,4096]{2,1,0:T(8,128)(2,1)S(1)} all-to-all(bf16[8,32,4096]{2,1,0:T(8,128)(2,1)S(1)} %stack.3), channel_id=1, replica_groups=mesh['ctx'=8,'head'=4] {'ctx'}, dimensions={0} | all-to-all | bytes 4194304 | tf_op jit(solution)/shard_map/all_to_all | solution.py:91
  287.5 0.0 copy-start.1
  287.5 28.5 %all_to_all.93 = bf16[4,64,4096]{2,1,0:T(8,128)(2,1)S(1)} all-to-all(bf16[4,64,4096]{2,1,0:T(8,128)(2,1)S(1)} %bitcast.65), channel_id=1, replica_groups=mesh['ctx'=8,'head'=4] {'head'}, dimensions={0} | all-to-all | bytes 4194304 | tf_op jit(solution)/shard_map/all_to_all | solution.py:93
  316.0 1.5 copy.89
  317.4 0.0 copy-done.1
  (5 shorter events, 0.0 us)
Async XLA Ops:
  0.0 58.0 %copy-start = (bf16[512,512]{1,0:T(8,128)(2,1)S(1)}, bf16[512,512]{1,0:T(8,128)(2,1)}, u32[]{:S(2)}) copy-start(bf16[512,512]{1,0:T(8,128)(2,1)} %param.10) | copy-start | bytes 1572868
  2.4 18.7 %all-to-all-start.1 = ((bf16[64,4,2048]{2,0,1:T(8,128)(2,1)}), bf16[64,4,2048]{2,0,1:T(8,128)(2,1)S(1)}, u32[]{:S(2)}, u32[]{:S(2)}) async-start(bf16[64,4,2048]{2,0,1:T(8,128)(2,1)} %bitcast.63), calls=%async_computation.1 | async-start | bytes 2097152 | tf_op jit(solution)/shard_map/all_to_all | solution.py:22
  6.7 18.9 %copy-start.5 = (s32[32,2]{0,1:T(2,128)S(1)}, s32[32,2]{0,1:T(2,128)}, u32[]{:S(2)}) copy-start(s32[32,2]{0,1:T(2,128)} %param.15) | copy-start | bytes 772
  6.7 18.9 %copy-start.4 = (s32[32,2,16]{0,2,1:T(8,128)S(1)}, s32[32,2,16]{0,2,1:T(8,128)}, u32[]{:S(2)}) copy-start(s32[32,2,16]{0,2,1:T(8,128)} %param.14) | copy-start | bytes 12292
  21.1 8.9 %copy-start.2 = (bf16[64,4,2048]{2,0,1:T(8,128)(2,1)}, bf16[64,4,2048]{2,0,1:T(8,128)(2,1)S(1)}, u32[]{:S(2)}) copy-start(bf16[64,4,2048]{2,0,1:T(8,128)(2,1)S(1)} %all-to-all-done.1) | copy-start | bytes 3145732
  21.1 34.8 %all-to-all-start = ((bf16[64,4,4096]{2,0,1:T(8,128)(2,1)}), bf16[64,4,4096]{2,0,1:T(8,128)(2,1)}, u32[]{:S(2)}, u32[]{:S(2)}) async-start(bf16[64,4,4096]{2,0,1:T(8,128)(2,1)} %bitcast.62), calls=%async_computation | async-start | bytes 4194304 | tf_op jit(solution)/shard_map/all_to_all | solution.py:21
  30.0 17.9 %copy-start.3 = (bf16[64,512]{1,0:T(8,128)(2,1)S(1)}, bf16[64,512]{1,0:T(8,128)(2,1)}, u32[]{:S(2)}) copy-start(bf16[64,512]{1,0:T(8,128)(2,1)} %param.11) | copy-start | bytes 196612
  87.8 21.2 %all-to-all-start.4 = ((f32[8,1,1024]{2,1,0:T(1,128)}), f32[8,1,1024]{2,1,0:T(1,128)S(1)}, u32[]{:S(2)}, u32[]{:S(2)}) async-start(f32[8,1,1024]{2,1,0:T(1,128)} %reshape.117), calls=%async_computation.4 | async-start | bytes 65536 | tf_op jit(solution)/shard_map/all_to_all | solution.py:78
  109.0 23.5 %all-to-all-start.3 = ((f32[8,1,1024]{2,1,0:T(1,128)}), f32[8,1,1024]{2,1,0:T(1,128)S(1)}, u32[]{:S(2)}, u32[]{:S(2)}) async-start(f32[8,1,1024]{2,1,0:T(1,128)} %reshape.115), calls=%async_computation.3 | async-start | bytes 65536 | tf_op jit(solution)/shard_map/all_to_all | solution.py:79
  132.6 98.7 %all-to-all-start.2 = ((f32[1,256,32,128]{3,2,0,1:T(8,128)}), f32[1,256,32,128]{3,2,0,1:T(8,128)}, u32[]{:S(2)}, u32[]{:S(2)}) async-start(f32[1,256,32,128]{3,2,0,1:T(8,128)} %copy.76), calls=%async_computation.2 | async-start | bytes 8388608 | tf_op jit(solution)/shard_map/all_to_all | solution.py:77
  287.5 30.0 %copy-start.1 = (bf16[512,512]{1,0:T(8,128)(2,1)S(1)}, bf16[512,512]{1,0:T(8,128)(2,1)}, u32[]{:S(2)}) copy-start(bf16[512,512]{1,0:T(8,128)(2,1)} %param.10) | copy-start | bytes 1572868
